TPU v7x, 32 devices: a whole 2x2x4 slice. The times are simulated.
32 devices in a mesh: parts: 2 (over y), space: 16 (over z, x, core).
Axes of the slice: x: 2, y: 2, z: 4, core: 2. Of those that a mesh axis runs over, the one named last changes fastest.
Arguments:
- snapshots: bfloat16 [2176, 8192], P('space', 'parts'), parts along dimension 1
- starts: int32 [16], replicated, may hold values from 0 to 1920, as said below
- bins: int32 [32], replicated, may hold values from 0 to 128
- mode_count: int32 [32], replicated, may hold values from 4 to 16
Outputs:
- modes: bfloat16 [32, 32, 8192], P(None, None, ('parts', 'space')), parts along dimension 2
- factor: float32 [64, 32, 32], P('parts'), parts along dimension 0
There are 2 independent parts, one for each index of `parts`. A program takes and returns all parts, laid end to end along the dimension named above; an argument that names none is the same for every part. Nothing has to cross between parts.
Inputs may be any that keep to these rules, and one draw needn't show every extreme that they name: Block starts rise; the first block starts at 0, the last at 1920, and successive starts differ by 64 to 192 snapshots.
All inputs are finite; a program needn't handle non-finite values.
Results may differ from a plain program's by a relative error of at most 0.008.
Values may be sent and summed in bfloat16 or wider, within the bound.
No kernel may reach another device: no remote copies, remote signals or barrier semaphores. Data moves between devices by JAX's collectives and lax.ppermute only.
A program may use at most 64 MiB of HBM per device.

v0:
```python
import math
import jax
import jax.numpy as jnp
from jax import lax
from jax.sharding import PartitionSpec as P

NB = 16
NWIN = 256
NFREQ = 32


def make_table(bins):
    offsets = jnp.arange(NWIN, dtype=jnp.int32)
    window = 0.5 - 0.5 * jnp.cos(2.0 * math.pi * offsets.astype(jnp.float32) / NWIN)
    scaling = 1.0 / jnp.sqrt(jnp.sum(window * window))
    turns = bins[:, None] * offsets[None, :] % NWIN
    phases = 2.0 * math.pi * turns.astype(jnp.float32) / NWIN
    cos_rows = scaling * window[None, :] * jnp.cos(phases)
    sin_rows = -scaling * window[None, :] * jnp.sin(phases)
    return jnp.concatenate([cos_rows, sin_rows], axis=0).astype(jnp.bfloat16)


def on_device(snapshots, starts, bins, mode_count):
    time_dev, all_points = snapshots.shape
    groups = lax.axis_size("space")
    points_dev = all_points // groups
    fourier_table = make_table(bins)
    arranged = snapshots.reshape(time_dev, groups, points_dev)
    series = lax.all_to_all(arranged, "space", split_axis=1, concat_axis=0, tiled=True)[:, 0, :]
    time_mean = jnp.mean(series.astype(jnp.float32), axis=0)
    centered = (series.astype(jnp.float32) - time_mean[None, :]).astype(jnp.bfloat16)

    def take_block(first):
        return lax.dynamic_slice_in_dim(centered, first, NWIN, 0)

    welch_windows = jax.vmap(take_block)(starts)
    matrix_product = jnp.einsum(
        "vx,oxy->voy", fourier_table, welch_windows, preferred_element_type=jnp.float32
    )
    spectra = matrix_product.astype(jnp.bfloat16)
    real_component = spectra[:NFREQ]
    imag_part = spectra[NFREQ:]
    stacked = jnp.concatenate([real_component, imag_part], axis=1)
    local_gram = jnp.einsum("fip,fjp->fij", stacked, stacked, preferred_element_type=jnp.float32)
    gram = lax.psum(local_gram, "space")
    real_real = gram[:, :NB, :NB]
    real_imag = gram[:, :NB, NB:]
    imag_real = gram[:, NB:, :NB]
    imag_imag = gram[:, NB:, NB:]
    summed = real_real + imag_imag
    skew_part = real_imag - imag_real
    upper_rows = jnp.concatenate([summed, -skew_part], axis=2)
    lower_rows = jnp.concatenate([skew_part, summed], axis=2)
    cross = jnp.concatenate([upper_rows, lower_rows], axis=1) / jnp.float32(all_points)
    lower_cholesky_matrix = jnp.linalg.cholesky(cross)
    signed = jnp.concatenate([real_component, -imag_part], axis=1).astype(jnp.float32)

    def solve_one(matrix, values):
        return jax.scipy.linalg.solve_triangular(matrix, values, lower=True)

    basis = jax.vmap(solve_one)(lower_cholesky_matrix, signed)
    row_index = jnp.arange(2 * NB, dtype=jnp.int32) % NB
    keep = row_index[None, :, None] < mode_count[:, None, None]
    modes = jnp.where(keep, basis, jnp.zeros_like(basis)).astype(jnp.bfloat16)
    factor = jnp.swapaxes(lower_cholesky_matrix, 1, 2)
    return (modes, factor)


def solution(mesh):
    in_specs = (P("space", "parts"), P(), P(), P())
    out_specs = (P(None, None, ("parts", "space")), P("parts", None, None))
    return jax.shard_map(
        on_device, mesh=mesh, in_specs=in_specs, out_specs=out_specs, check_vma=False
    )
```

profile of v0, /device:TPU:1, one launch (start us, length us, event | category | flops | bytes accessed | tf_op | source)
XLA Modules:
  0.0 287.9 jit_solution(15959052177133936224)
XLA Ops:
  7.2 2.4 copy.33
  9.5 7.3 %all-to-all-start = ((bf16[136,16,256]{2,0,1:T(8,128)(2,1)}), bf16[136,16,256]{2,0,1:T(8,128)(2,1)S(1)}, u32[]{:S(2)}, u32[]{:S(2)}) async-start(bf16[136,16,256]{2,0,1:T(8,128)(2,1)} %bitcast.30), calls=%async_computation | async-start | bytes 2228224 | tf_op jit(solution)/shard_map/all_to_all | solution.py:29
  16.9 0.6 multiply_reduce_fusion
  18.7 22.5 %all-to-all-done = bf16[136,16,256]{2,0,1:T(8,128)(2,1)S(1)} async-done(((bf16[136,16,256]{2,0,1:T(8,128)(2,1)}), bf16[136,16,256]{2,0,1:T(8,128)(2,1)S(1)}, u32[]{:S(2)}, u32[]{:S(2)}) %all-to-all-start) | async-done | bytes 1114144 | tf_op jit(solution)/shard_map/all_to_all | solution.py:29
  41.2 0.3 convert_reduce_fusion
  41.8 30.8 %while.1 = (s32[]{:T(128)}, bf16[2176,256]{1,0:T(8,128)(2,1)S(1)}, s32[16,2]{0,1:T(2,128)S(1)}, bf16[16,256,256]{2,1,0:T(8,128)(2,1)}, s32[]{:T(128)}) while((s32[]{:T(128)}, bf16[2176,256]{1,0:T(8,128)(2,1)S(1)}, s32[16,2]{0,1:T(2,128)S(1)}, bf16[16,256,256]{2,1,0:T(8,128)(2,1)}, s32[]{:T(128)}) %tuple.30), condition=%wide.while_cond, body=%wide.while_body.sunk | while | flops 2 | bytes 262757 | solution.py:34
  41.8 0.5 slice.63
  42.4 1.3 bitcast_dynamic-update-slice_fusion.2
  43.8 0.5 slice.63
  44.3 1.3 bitcast_dynamic-update-slice_fusion.2
  45.7 0.5 slice.63
  46.2 1.3 bitcast_dynamic-update-slice_fusion.2
  47.6 0.5 slice.63
  48.1 1.3 bitcast_dynamic-update-slice_fusion.2
  49.5 0.5 slice.63
  50.0 1.3 bitcast_dynamic-update-slice_fusion.2
  51.4 0.5 slice.63
  52.0 1.3 bitcast_dynamic-update-slice_fusion.2
  53.4 0.5 slice.63
  53.9 1.3 bitcast_dynamic-update-slice_fusion.2
  55.3 0.5 slice.63
  55.8 1.3 bitcast_dynamic-update-slice_fusion.2
  57.2 0.5 slice.63
  57.7 1.3 bitcast_dynamic-update-slice_fusion.2
  59.2 0.5 slice.63
  59.7 1.3 bitcast_dynamic-update-slice_fusion.2
  61.1 0.5 slice.63
  61.6 1.3 bitcast_dynamic-update-slice_fusion.2
  63.0 0.5 slice.63
  63.5 1.3 bitcast_dynamic-update-slice_fusion.2
  64.9 0.5 slice.63
  65.5 1.3 bitcast_dynamic-update-slice_fusion.2
  66.9 0.5 slice.63
  67.4 1.3 bitcast_dynamic-update-slice_fusion.2
  68.8 0.5 slice.63
  69.3 1.3 bitcast_dynamic-update-slice_fusion.2
  70.7 0.5 slice.63
  71.2 1.3 bitcast_dynamic-update-slice_fusion.2
  72.6 2.1 convolution_convert_fusion
  74.8 1.2 fusion.4
  76.0 92.4 %all-reduce.3.cloned.1.call-done = f32[32,32,32]{1,2,0:T(8,128)} async-done(((f32[32,32,32]{1,2,0:T(8,128)}), f32[32,32,32]{1,2,0:T(8,128)}) %all-reduce.3.cloned.1.call-update) | async-done | bytes 131088 | tf_op jit(solution)/shard_map/psum | solution.py:45
  168.5 1.4 fusion.17
  170.5 93.8 %custom-call.8 = f32[32,32,32]{2,1,0:T(8,128)S(1)} custom-call(f32[32,32,32]{2,1,0:T(8,128)S(1)} %fusion.2), custom_call_target="Cholesky" | custom-call | tf_op jit(solution)/shard_map/jit(cholesky)/cholesky | solution.py:55
  264.2 0.3 copy.21
  265.0 12.5 %custom-call.9 = f32[32,1,32,32]{0,2,3,1:T(8,128)S(1)} custom-call(f32[32,1,32,32]{0,3,2,1:T(8,128)S(1)} %get-tuple-element.25), custom_call_target="InvertDiagBlocksLowerTriangular" | custom-call | tf_op jit(solution)/shard_map/vmap(jit(_solve_triangular))/triangular_solve | solution.py:59
  277.5 0.6 copy.23
  278.1 1.3 copy.25
  279.4 1.6 fusion.1
  (43 shorter events, 3.0 us)
Async XLA Ops:
  7.2 11.1 %copy-start.2 = (s32[16]{0:T(128)S(1)}, s32[16]{0:T(128)}, u32[]{:S(2)}) copy-start(s32[16]{0:T(128)} %param.5) | copy-start | bytes 196
  7.2 11.2 %copy-start.1 = (s32[32]{0:T(128)S(1)}, s32[32]{0:T(128)}, u32[]{:S(2)}) copy-start(s32[32]{0:T(128)} %param.7) | copy-start | bytes 388
  7.2 11.3 %copy-start = (s32[32]{0:T(128)S(1)}, s32[32]{0:T(128)}, u32[]{:S(2)}) copy-start(s32[32]{0:T(128)} %param.6) | copy-start | bytes 388
  9.5 31.7 %all-to-all-start = ((bf16[136,16,256]{2,0,1:T(8,128)(2,1)}), bf16[136,16,256]{2,0,1:T(8,128)(2,1)S(1)}, u32[]{:S(2)}, u32[]{:S(2)}) async-start(bf16[136,16,256]{2,0,1:T(8,128)(2,1)} %bitcast.30), calls=%async_computation | async-start | bytes 2228224 | tf_op jit(solution)/shard_map/all_to_all | solution.py:29
  16.9 151.6 %all-reduce.3.cloned.1.call-start = ((), (), s32[]{:S(2)}) async-start(), calls=%async_computation.1 | async-start | bytes 1048576 | tf_op jit(solution)/shard_map/psum | solution.py:45
Sparse Core Ops, SparseCore 0:
  76.1 92.2 all-reduce.2
where the time goes:
time: 288 us
  waiting for transfers between devices  115 us (40%)
  other arithmetic  110 us (38%)
  local copies, waits for them, and re-layouts  35.5 us (12%)
  between operations  14.9 us (5%)
  starting transfers between devices  7.36 us (3%)
  matrix products  4.92 us (2%)
    another operation x4, other arithmetic, on_device(): lower_cholesky_matrix = jnp.linalg.cholesky(cross)  94 us
    psum x1, waiting for transfers between devices, on_device(): gram = lax.psum(local_gram, 'space')  92.4 us
    gather x48, local copies, waits for them, and re-layouts  30.8 us
    all_to_all x1, waiting for transfers between devices, on_device(): lax.all_to_all(arranged, 'space', split_axis=1, concat_axis=0, tiled=True)  22.5 us
    another operation x2, other arithmetic, solve_one(): return jax.scipy.linalg.solve_triangular(matrix, values, lower=True)  12.5 us
    all_to_all x1, starting transfers between devices, on_device(): lax.all_to_all(arranged, 'space', split_axis=1, concat_axis=0, tiled=True)  7.32 us
  transfers between devices with their start and end apart: 2, of which 2 were waited for; matrix products, arithmetic and copies ran while one was open for 0% of the time, Pallas kernels for 0%

commit v1 on v0

--- a/solution.py
+++ b/solution.py
@@ -26,7 +26,12 @@
     points_dev = all_points // groups
     fourier_table = make_table(bins)
     arranged = snapshots.reshape(time_dev, groups, points_dev)
-    series = lax.all_to_all(arranged, "space", split_axis=1, concat_axis=0, tiled=True)[:, 0, :]
+    series = jnp.concatenate(
+        lax.all_to_all(
+            jnp.stack(jnp.split(arranged, lax.axis_size("space"), axis=1)), "space", 0, 0
+        ),
+        axis=0,
+    )[:, 0, :]
     time_mean = jnp.mean(series.astype(jnp.float32), axis=0)
     centered = (series.astype(jnp.float32) - time_mean[None, :]).astype(jnp.bfloat16)
 

time: 288 us -> 299 us (1.038)
  local copies, waits for them, and re-layouts: 35.5 us -> 46.5 us
    unnamed x7 -> x23, local copies, waits for them, and re-layouts: 1.33 us -> 12.3 us
where the time goes in v1:
time: 299 us
  waiting for transfers between devices  115 us (38%)
  other arithmetic  110 us (37%)
  local copies, waits for them, and re-layouts  46.5 us (16%)
  between operations  14.9 us (5%)
  starting transfers between devices  7.49 us (3%)
  matrix products  4.92 us (2%)
    another operation x4, other arithmetic, on_device(): lower_cholesky_matrix = jnp.linalg.cholesky(cross)  94 us
    psum x1, waiting for transfers between devices, on_device(): gram = lax.psum(local_gram, 'space')  92.4 us
    gather x48, local copies, waits for them, and re-layouts  30.7 us
    all_to_all x1, waiting for transfers between devices, on_device(): lax.all_to_all(jnp.stack(jnp.split(arranged, lax.axis_size('space'), axis...  22.5 us
    another operation x2, other arithmetic, solve_one(): return jax.scipy.linalg.solve_triangular(matrix, values, lower=True)  12.5 us
    unnamed x23, local copies, waits for them, and re-layouts  12.3 us
    all_to_all x1, starting transfers between devices, on_device(): lax.all_to_all(jnp.stack(jnp.split(arranged, lax.axis_size('space'), axis...  7.45 us
  transfers between devices with their start and end apart: 2, of which 2 were waited for; matrix products, arithmetic and copies ran while one was open for 0% of the time, Pallas kernels for 0%

profile of v1, /device:TPU:1, one launch (start us, length us, event | category | flops | bytes accessed | tf_op | source)
XLA Modules:
  0.0 299.0 jit_solution(11118423231322477086)
XLA Ops:
  7.2 1.5 copy.330
  8.7 1.8 fusion.18
  10.5 0.6 bitcast_dynamic-update-slice_fusion.16
  11.2 0.6 bitcast_dynamic-update-slice_fusion.15
  11.8 0.6 bitcast_dynamic-update-slice_fusion.14
  12.4 0.6 bitcast_dynamic-update-slice_fusion.13
  13.1 0.6 bitcast_dynamic-update-slice_fusion.12
  13.7 0.6 bitcast_dynamic-update-slice_fusion.11
  14.3 0.6 bitcast_dynamic-update-slice_fusion.10
  14.9 0.6 bitcast_dynamic-update-slice_fusion.9
  15.6 0.6 bitcast_dynamic-update-slice_fusion.8
  16.2 0.6 bitcast_dynamic-update-slice_fusion.7
  16.8 0.6 bitcast_dynamic-update-slice_fusion.6
  17.5 0.6 bitcast_dynamic-update-slice_fusion.5
  18.1 0.6 bitcast_dynamic-update-slice_fusion.4
  18.7 0.6 bitcast_dynamic-update-slice_fusion.3
  19.4 0.6 bitcast_dynamic-update-slice_fusion.2
  20.0 0.6 bitcast_dynamic-update-slice_fusion.1
  20.6 7.5 %all-to-all-start = ((bf16[16,136,1,256]{3,1,2,0:T(8,128)(2,1)}), bf16[16,136,1,256]{3,1,2,0:T(8,128)(2,1)S(1)}, u32[]{:S(2)}, u32[]{:S(2)}) async-start(bf16[16,136,1,256]{3,1,2,0:T(8,128)(2,1)} %bitcast_dynamic-update-slice_fusion.1), calls=%async_computation | async-start | bytes 2228224 | tf_op jit(solution)/shard_map/all_to_all | solution.py:30
  28.1 0.6 multiply_reduce_fusion
  29.9 22.5 %all-to-all-done = bf16[16,136,1,256]{3,1,2,0:T(8,128)(2,1)S(1)} async-done(((bf16[16,136,1,256]{3,1,2,0:T(8,128)(2,1)}), bf16[16,136,1,256]{3,1,2,0:T(8,128)(2,1)S(1)}, u32[]{:S(2)}, u32[]{:S(2)}) %all-to-all-start) | async-done | bytes 1114144 | tf_op jit(solution)/shard_map/all_to_all | solution.py:30
  53.0 30.7 %while.1 = (s32[]{:T(128)}, bf16[2176,256]{1,0:T(8,128)(2,1)S(1)}, s32[16,2]{0,1:T(2,128)S(1)}, bf16[16,256,256]{2,1,0:T(8,128)(2,1)}, s32[]{:T(128)}) while((s32[]{:T(128)}, bf16[2176,256]{1,0:T(8,128)(2,1)S(1)}, s32[16,2]{0,1:T(2,128)S(1)}, bf16[16,256,256]{2,1,0:T(8,128)(2,1)}, s32[]{:T(128)}) %tuple.62), condition=%wide.while_cond, body=%wide.while_body.sunk | while | flops 2 | bytes 263257 | solution.py:39
  53.1 0.5 slice.63
  53.6 1.3 bitcast_dynamic-update-slice_fusion.18
  55.5 1.3 bitcast_dynamic-update-slice_fusion.18
  57.4 1.3 bitcast_dynamic-update-slice_fusion.18
  59.3 1.3 bitcast_dynamic-update-slice_fusion.18
  61.2 1.3 bitcast_dynamic-update-slice_fusion.18
  63.2 1.3 bitcast_dynamic-update-slice_fusion.18
  65.1 1.3 bitcast_dynamic-update-slice_fusion.18
  67.0 1.3 bitcast_dynamic-update-slice_fusion.18
  68.9 1.3 bitcast_dynamic-update-slice_fusion.18
  70.8 1.3 bitcast_dynamic-update-slice_fusion.18
  72.8 1.3 bitcast_dynamic-update-slice_fusion.18
  74.7 1.3 bitcast_dynamic-update-slice_fusion.18
  76.6 1.3 bitcast_dynamic-update-slice_fusion.18
  78.5 1.3 bitcast_dynamic-update-slice_fusion.18
  80.4 1.3 bitcast_dynamic-update-slice_fusion.18
  82.4 1.3 bitcast_dynamic-update-slice_fusion.18
  83.7 2.1 convolution_convert_fusion
  85.9 1.2 fusion.4
  87.2 92.4 %all-reduce.3.cloned.1.call-done = f32[32,32,32]{1,2,0:T(8,128)} async-done(((f32[32,32,32]{1,2,0:T(8,128)}), f32[32,32,32]{1,2,0:T(8,128)}) %all-reduce.3.cloned.1.call-update) | async-done | bytes 131088 | tf_op jit(solution)/shard_map/psum | solution.py:50
  179.6 1.4 fusion.17
  181.6 93.8 %custom-call.8 = f32[32,32,32]{2,1,0:T(8,128)S(1)} custom-call(f32[32,32,32]{2,1,0:T(8,128)S(1)} %fusion.2), custom_call_target="Cholesky" | custom-call | tf_op jit(solution)/shard_map/jit(cholesky)/cholesky | solution.py:60
  276.2 12.5 %custom-call.9 = f32[32,1,32,32]{0,2,3,1:T(8,128)S(1)} custom-call(f32[32,1,32,32]{0,3,2,1:T(8,128)S(1)} %get-tuple-element.75), custom_call_target="InvertDiagBlocksLowerTriangular" | custom-call | tf_op jit(solution)/shard_map/vmap(jit(_solve_triangular))/triangular_solve | solution.py:64
  288.7 0.6 copy.310
  289.2 1.3 copy.312
  290.5 1.6 fusion.1
  (60 shorter events, 11.4 us)
Async XLA Ops:
  20.6 8.9 %copy-start.2 = (s32[16]{0:T(128)S(1)}, s32[16]{0:T(128)}, u32[]{:S(2)}) copy-start(s32[16]{0:T(128)} %param.5) | copy-start | bytes 196
  20.6 9.0 %copy-start.1 = (s32[32]{0:T(128)S(1)}, s32[32]{0:T(128)}, u32[]{:S(2)}) copy-start(s32[32]{0:T(128)} %param.7) | copy-start | bytes 388
  20.6 9.0 %copy-start = (s32[32]{0:T(128)S(1)}, s32[32]{0:T(128)}, u32[]{:S(2)}) copy-start(s32[32]{0:T(128)} %param.6) | copy-start | bytes 388
  20.6 31.8 %all-to-all-start = ((bf16[16,136,1,256]{3,1,2,0:T(8,128)(2,1)}), bf16[16,136,1,256]{3,1,2,0:T(8,128)(2,1)S(1)}, u32[]{:S(2)}, u32[]{:S(2)}) async-start(bf16[16,136,1,256]{3,1,2,0:T(8,128)(2,1)} %bitcast_dynamic-update-slice_fusion.1), calls=%async_computation | async-start | bytes 2228224 | tf_op jit(solution)/shard_map/all_to_all | solution.py:30
  28.1 151.5 %all-reduce.3.cloned.1.call-start = ((), (), s32[]{:S(2)}) async-start(), calls=%async_computation.1 | async-start | bytes 1048576 | tf_op jit(solution)/shard_map/psum | solution.py:50
Sparse Core Ops, SparseCore 0:
  87.3 92.2 all-reduce.2

commit v2 on v0

--- a/solution.py
+++ b/solution.py
@@ -42,7 +42,7 @@
     imag_part = spectra[NFREQ:]
     stacked = jnp.concatenate([real_component, imag_part], axis=1)
     local_gram = jnp.einsum("fip,fjp->fij", stacked, stacked, preferred_element_type=jnp.float32)
-    gram = lax.psum(local_gram, "space")
+    gram = jnp.sum(lax.all_gather(local_gram, "space"), axis=0)
     real_real = gram[:, :NB, :NB]
     real_imag = gram[:, :NB, NB:]
     imag_real = gram[:, NB:, :NB]

time: 288 us -> 277 us (0.962)
  waiting for transfers between devices: 115 us -> 99.6 us
  other arithmetic: 110 us -> 113 us
    psum x1 -> x0, waiting for transfers between devices: 92.4 us -> none  [on_device(): gram = lax.psum(local_gram, 'space')]
    all_gather x0 -> x1, waiting for transfers between devices: none -> 77 us  [on_device(): gram = jnp.sum(lax.all_gather(local_gram, 'space'), axis=0)]
    reduce_sum x0 -> x1, other arithmetic: none -> 4.49 us  [on_device(): gram = jnp.sum(lax.all_gather(local_gram, 'space'), axis=0)]
where the time goes in v2:
time: 277 us; the launch traced here: 276 us
  other arithmetic  113 us (41%)
  waiting for transfers between devices  99.6 us (36%)
  local copies, waits for them, and re-layouts  36.1 us (13%)
  between operations  14.9 us (5%)
  starting transfers between devices  7.36 us (3%)
  matrix products  4.91 us (2%)
    another operation x4, other arithmetic, on_device(): lower_cholesky_matrix = jnp.linalg.cholesky(cross)  94 us
    all_gather x1, waiting for transfers between devices, on_device(): gram = jnp.sum(lax.all_gather(local_gram, 'space'), axis=0)  77 us
    gather x48, local copies, waits for them, and re-layouts  30.7 us
    all_to_all x1, waiting for transfers between devices, on_device(): lax.all_to_all(arranged, 'space', split_axis=1, concat_axis=0, tiled=True)  22.6 us
    another operation x2, other arithmetic, solve_one(): return jax.scipy.linalg.solve_triangular(matrix, values, lower=True)  12.5 us
    all_to_all x1, starting transfers between devices, on_device(): lax.all_to_all(arranged, 'space', split_axis=1, concat_axis=0, tiled=True)  7.32 us
  transfers between devices with their start and end apart: 2, of which 2 were waited for; matrix products, arithmetic and copies ran while one was open for 0% of the time, Pallas kernels for 0%

profile of v2, /device:TPU:1, one launch (start us, length us, event | category | flops | bytes accessed | tf_op | source)
XLA Modules:
  0.0 276.3 jit_solution(13360002624750411451)
XLA Ops:
  7.2 2.3 copy.38
  9.5 7.3 %all-to-all-start = ((bf16[136,16,256]{2,0,1:T(8,128)(2,1)}), bf16[136,16,256]{2,0,1:T(8,128)(2,1)S(1)}, u32[]{:S(2)}, u32[]{:S(2)}) async-start(bf16[136,16,256]{2,0,1:T(8,128)(2,1)} %bitcast.31), calls=%async_computation | async-start | bytes 2228224 | tf_op jit(solution)/shard_map/all_to_all | solution.py:29
  16.9 0.6 multiply_reduce_fusion
  18.5 22.6 %all-to-all-done = bf16[136,16,256]{2,0,1:T(8,128)(2,1)S(1)} async-done(((bf16[136,16,256]{2,0,1:T(8,128)(2,1)}), bf16[136,16,256]{2,0,1:T(8,128)(2,1)S(1)}, u32[]{:S(2)}, u32[]{:S(2)}) %all-to-all-start) | async-done | bytes 1114144 | tf_op jit(solution)/shard_map/all_to_all | solution.py:29
  41.2 0.3 convert_reduce_fusion
  41.7 30.7 %while.1 = (s32[]{:T(128)}, bf16[2176,256]{1,0:T(8,128)(2,1)S(1)}, s32[16,2]{0,1:T(2,128)S(1)}, bf16[16,256,256]{2,1,0:T(8,128)(2,1)}, s32[]{:T(128)}) while((s32[]{:T(128)}, bf16[2176,256]{1,0:T(8,128)(2,1)S(1)}, s32[16,2]{0,1:T(2,128)S(1)}, bf16[16,256,256]{2,1,0:T(8,128)(2,1)}, s32[]{:T(128)}) %tuple.32), condition=%wide.while_cond, body=%wide.while_body.sunk | while | flops 2 | bytes 263257 | solution.py:34
  41.8 0.5 slice.61
  42.3 1.3 bitcast_dynamic-update-slice_fusion.2
  43.7 0.5 slice.61
  44.2 1.3 bitcast_dynamic-update-slice_fusion.2
  45.6 0.5 slice.61
  46.2 1.3 bitcast_dynamic-update-slice_fusion.2
  47.6 0.5 slice.61
  48.1 1.3 bitcast_dynamic-update-slice_fusion.2
  49.5 0.5 slice.61
  50.0 1.3 bitcast_dynamic-update-slice_fusion.2
  51.4 0.5 slice.61
  51.9 1.3 bitcast_dynamic-update-slice_fusion.2
  53.3 0.5 slice.61
  53.8 1.3 bitcast_dynamic-update-slice_fusion.2
  55.2 0.5 slice.61
  55.7 1.3 bitcast_dynamic-update-slice_fusion.2
  57.1 0.5 slice.61
  57.7 1.3 bitcast_dynamic-update-slice_fusion.2
  59.1 0.5 slice.61
  59.6 1.3 bitcast_dynamic-update-slice_fusion.2
  61.0 0.5 slice.61
  61.5 1.3 bitcast_dynamic-update-slice_fusion.2
  62.9 0.5 slice.61
  63.4 1.3 bitcast_dynamic-update-slice_fusion.2
  64.8 0.5 slice.61
  65.3 1.3 bitcast_dynamic-update-slice_fusion.2
  66.8 0.5 slice.61
  67.3 1.3 bitcast_dynamic-update-slice_fusion.2
  68.7 0.5 slice.61
  69.2 1.3 bitcast_dynamic-update-slice_fusion.2
  70.6 0.5 slice.61
  71.1 1.3 bitcast_dynamic-update-slice_fusion.2
  72.4 2.1 convolution_convert_fusion
  74.7 1.2 fusion.4
  76.0 77.0 %all-gather.3.cloned.1.call-done = f32[512,32,32]{2,1,0:T(8,128)} async-done(((f32[32,32,32]{2,1,0:T(8,128)}), f32[512,32,32]{2,1,0:T(8,128)}) %all-gather.3.cloned.1.call-update) | async-done | bytes 2097168 | tf_op jit(solution)/shard_map/all_gather | solution.py:45
  153.0 4.5 %reduce_sum.29 = f32[32,32,32]{2,1,0:T(8,128)S(1)} reduce(f32[16,32,32,32]{3,2,1,0:T(8,128)} %bitcast.36, f32[]{:T(128)} %constant.92.clone.1), dimensions={0}, to_apply=%region_2.3 | reduce | flops 491520 | bytes 2228228 | tf_op jit(solution)/shard_map/reduce_sum | solution.py:45
  159.0 93.8 %custom-call.8 = f32[32,32,32]{2,1,0:T(8,128)S(1)} custom-call(f32[32,32,32]{2,1,0:T(8,128)S(1)} %fusion.2), custom_call_target="Cholesky" | custom-call | tf_op jit(solution)/shard_map/jit(cholesky)/cholesky | solution.py:55
  252.7 0.3 copy.23
  253.5 12.5 %custom-call.9 = f32[32,1,32,32]{0,2,3,1:T(8,128)S(1)} custom-call(f32[32,1,32,32]{0,3,2,1:T(8,128)S(1)} %get-tuple-element.25), custom_call_target="InvertDiagBlocksLowerTriangular" | custom-call | tf_op jit(solution)/shard_map/vmap(jit(_solve_triangular))/triangular_solve | solution.py:59
  266.0 0.6 copy.25
  266.5 1.3 copy.27
  267.9 1.6 fusion.1
  (50 shorter events, 3.8 us)
Async XLA Ops:
  7.2 11.1 %copy-start.2 = (s32[16]{0:T(128)S(1)}, s32[16]{0:T(128)}, u32[]{:S(2)}) copy-start(s32[16]{0:T(128)} %param.5) | copy-start | bytes 196
  7.2 11.2 %copy-start = (s32[32]{0:T(128)S(1)}, s32[32]{0:T(128)}, u32[]{:S(2)}) copy-start(s32[32]{0:T(128)} %param.6) | copy-start | bytes 388
  9.5 31.7 %all-to-all-start = ((bf16[136,16,256]{2,0,1:T(8,128)(2,1)}), bf16[136,16,256]{2,0,1:T(8,128)(2,1)S(1)}, u32[]{:S(2)}, u32[]{:S(2)}) async-start(bf16[136,16,256]{2,0,1:T(8,128)(2,1)} %bitcast.31), calls=%async_computation | async-start | bytes 2228224 | tf_op jit(solution)/shard_map/all_to_all | solution.py:29
  16.8 136.2 %all-gather.3.cloned.1.call-start = ((), (), s32[]{:S(2)}) async-start(), calls=%async_computation.1 | async-start | bytes 8912896 | tf_op jit(solution)/shard_map/all_gather | solution.py:45
  74.5 1.4 copy-start.1
Sparse Core Ops, SparseCore 0:
  76.0 76.9 all-gather.2
